TPU v7x, 512 devices: a whole 4x8x8 slice. The times are simulated.
512 devices in a mesh: dom: 16 (over x_lo, y), gx: 4 (over x_hi, core), gy: 8 (over z).
Axes of the slice: x: 4 (x_hi: 2, x_lo: 2; x = x_hi * 2 + x_lo), y: 8, z: 8, core: 2. Of those that a mesh axis runs over, the one named last changes fastest.
Arguments:
- ensemble: float32 [16, 4, 32, 32, 1024], P('dom', None, None, 'gx', 'gy'), may hold values from -6 to 6
- ancestors: int32 [16, 4, 128], P(None, 'gx', 'gy'), may hold values from 0 to 15
- particle_air_drag: float32 [16, 2, 32, 1024], P('dom', None, 'gx', 'gy'), may hold values from -6 to 6
- eddy_diffusivity: float32 [31], replicated, may hold values from 0.02 to 0.15
Outputs:
- forecast: float32 [16, 4, 32, 32, 1024], P('dom', None, None, 'gx', 'gy')
All inputs are finite; a program needn't handle non-finite values.
Results may differ from a plain program's by a relative error of at most 0.0003.
Values sent between devices are 32-bit elements; how exact they have to be, the bound alone decides.
No kernel may reach another device: no remote copies, remote signals or barrier semaphores. Data moves between devices by JAX's collectives and lax.ppermute only.
A program may use at most 64 MiB of HBM per device.

v0:
```python
import jax
import jax.numpy as jnp
from jax import lax
from jax.sharding import PartitionSpec as P

STEPS = 4
TILE = 8
ADVECT = 0.2
DIFFUSE = 0.15
BUOY_TEMP = 0.2
BUOY_SALT = 0.1
PRESS_SCALE = 0.25
WIND_SCALE = 0.2
CORIO_BASE = 0.1
CORIO_SLOPE = 0.1


def extended(x, sides, width, wrap):
    for axis, dim in sides:
        size, length = (lax.axis_size(axis), x.shape[dim])
        up = [(i, (i + 1) % size) for i in range(size if wrap else size - 1)]
        down = [(j, i) for i, j in up]
        last = lax.slice_in_dim(x, length - width, length, axis=dim)
        leading = lax.slice_in_dim(x, 0, width, axis=dim)
        before = lax.ppermute(last, axis, up)
        after = lax.ppermute(leading, axis, down)
        x = jnp.concatenate([before, x, after], axis=dim)
    return x


def advance(padded, topmost_slab, eddy_diffusivity, coriolis):
    centre = padded[:, :, 1:-1, 1:-1]
    eastern_neighbour_cell = padded[:, :, 2:, 1:-1]
    west_cell = padded[:, :, :-2, 1:-1]
    north_cell = padded[:, :, 1:-1, 2:]
    south_cell = padded[:, :, 1:-1, :-2]
    grad_x = 0.5 * (eastern_neighbour_cell - west_cell)
    grad_y = 0.5 * (north_cell - south_cell)
    spread = eastern_neighbour_cell + west_cell + north_cell + south_cell - 4.0 * centre
    buoyancy = BUOY_TEMP * padded[2] - BUOY_SALT * padded[3]
    pressure = PRESS_SCALE * jnp.cumsum(buoyancy, axis=0)
    press_x = 0.5 * (pressure[:, 2:, 1:-1] - pressure[:, :-2, 1:-1])
    press_y = 0.5 * (pressure[:, 1:-1, 2:] - pressure[:, 1:-1, :-2])
    vert_flux = eddy_diffusivity[None, :, None, None] * (centre[:, 1:] - centre[:, :-1])
    closed = jnp.zeros_like(centre[:, :1])
    vertical = jnp.concatenate([vert_flux, closed], axis=1) - jnp.concatenate(
        [closed, vert_flux], axis=1
    )
    east_vel = centre[0]
    north_vel = centre[1]
    carried_over = east_vel[None] * grad_x + north_vel[None] * grad_y
    common = centre - ADVECT * carried_over + DIFFUSE * spread + vertical
    level_top = (jnp.arange(centre.shape[1]) == 0).astype(jnp.float32)[:, None, None]
    forcing = WIND_SCALE * topmost_slab[:, None] * level_top
    east_next = common[0] + coriolis * north_vel - press_x + forcing[0]
    north_next = common[1] - coriolis * east_vel - press_y + forcing[1]
    return jnp.stack([east_next, north_next, common[2], common[3]])


def coriolis_at(positions, total_rows):
    return CORIO_BASE + CORIO_SLOPE * (positions.astype(jnp.float32) + 0.5) / total_rows


def per_device(ensemble, ancestors, particle_air_drag, eddy_diffusivity):
    particle_number = lax.axis_index("dom")
    width_y = ensemble.shape[4]
    own_tiles = lax.dynamic_index_in_dim(ancestors, particle_number, 0, keepdims=False)
    cell_source = jnp.repeat(jnp.repeat(own_tiles, TILE, 0), TILE, 1)
    shards = lax.all_gather(ensemble, "dom", axis=0, tiled=True)

    def place(offset, partial_state):
        wanted = (cell_source == offset)[None, None]
        return jnp.where(wanted, shards[offset], partial_state)

    selected_particles = lax.fori_loop(
        0, shards.shape[0], place, jnp.zeros(ensemble.shape[1:], jnp.float32)
    )
    row_block = lax.axis_index("gy")
    total_rows = width_y * lax.axis_size("gy")
    topmost_slab = particle_air_drag[0]
    positions = row_block * width_y + jnp.arange(width_y, dtype=jnp.int32)
    coriolis = coriolis_at(positions, total_rows)
    marine_variables = selected_particles
    for iteration in range(STEPS):
        widened = extended(marine_variables, (("gx", 2),), 1, True)
        padded = extended(widened, (("gy", 3),), 1, False)
        marine_variables = advance(padded, topmost_slab, eddy_diffusivity, coriolis)
    return marine_variables[None]


def solution(mesh):
    placed = (
        P("dom", None, None, "gx", "gy"),
        P(None, "gx", "gy"),
        P("dom", None, "gx", "gy"),
        P(),
    )
    return jax.shard_map(
        per_device,
        mesh=mesh,
        in_specs=placed,
        out_specs=P("dom", None, None, "gx", "gy"),
        check_vma=False,
    )
```

profile of v0, /device:TPU:256, one launch (start us, length us, event | category | flops | bytes accessed | tf_op | source)
XLA Modules:
  0.0 242.3 jit_solution(3216205016897837042)
XLA Ops:
  6.5 0.7 all-gather.2.cloned.1.call-update
  7.5 0.7 multiply_bitcast_fusion
  8.3 106.1 %all-gather.2.cloned.1.call-done = f32[16,4,32,8,128]{4,3,2,1,0:T(8,128)} async-done(((f32[1,4,32,8,128]{4,3,2,1,0:T(8,128)}), f32[16,4,32,8,128]{4,3,2,1,0:T(8,128)}) %all-gather.2.cloned.1.call-update) | async-done | bytes 8388624 | tf_op jit(solution)/shard_map/all_gather | solution.py:69
  114.4 19.9 %while.14 = (s32[]{:T(128)}, f32[4,32,8,128]{3,2,1,0:T(8,128)S(1)}, f32[16,4,32,8,128]{4,3,2,1,0:T(8,128)}, s32[128]{0:T(128)S(1)}, s32[]{:T(128)}, /*index=5*/s32[]{:T(128)}) while((s32[]{:T(128)}, f32[4,32,8,128]{3,2,1,0:T(8,128)S(1)}, f32[16,4,32,8,128]{4,3,2,1,0:T(8,128)}, s32[128]{0:T(128)S(1)}, s32[]{:T(128)}, ...), condition=%wide.region_1.2_spmd.clone, body=%wide.region_0.1_spmd.clone.sunk | while | flops 262275 | bytes 1573719 | solution.py:75
  114.4 1.2 bitcast_select_fusion.2
  115.7 1.2 bitcast_select_fusion.2
  116.9 1.2 bitcast_select_fusion.2
  118.2 1.2 bitcast_select_fusion.2
  119.4 1.2 bitcast_select_fusion.2
  120.7 1.2 bitcast_select_fusion.2
  121.9 1.2 bitcast_select_fusion.2
  123.2 1.2 bitcast_select_fusion.2
  124.4 1.2 bitcast_select_fusion.2
  125.7 1.2 bitcast_select_fusion.2
  126.9 1.2 bitcast_select_fusion.2
  128.2 1.2 bitcast_select_fusion.2
  129.4 1.2 bitcast_select_fusion.2
  130.7 1.2 bitcast_select_fusion.2
  131.9 1.2 bitcast_select_fusion.2
  133.2 1.2 bitcast_select_fusion.2
  134.5 3.9 %collective-permute-start = (f32[4,32,1,128]{3,2,1,0:T(1,128)S(1)}, f32[4,32,1,128]{3,2,1,0:T(1,128)S(1)}, u32[]{:S(2)}, u32[]{:S(2)}) collective-permute-start(f32[4,32,1,128]{3,2,1,0:T(1,128)S(1)} %get-tuple-element.148), channel_id=1, source_target_pairs={{8,0},{16,8},{24,16},{0,24},{9,1},{17,9},{25,17},{1,25},{10,2},{18... | collective-permute-start | bytes 196616 | tf_op jit(solution)/shard_map/ppermute | solution.py:26
  138.3 1.9 collective-permute-start.1
  140.3 0.9 subtract_multiply_fusion
  141.2 4.3 %collective-permute-done.1 = f32[4,32,1,128]{3,2,1,0:T(1,128)S(1)} collective-permute-done((f32[4,32,1,128]{3,2,1,0:T(1,128)S(1)}, f32[4,32,1,128]{3,2,1,0:T(1,128)S(1)}, u32[]{:S(2)}, u32[]{:S(2)}) %collective-permute-start.1) | collective-permute-done | bytes 65568 | tf_op jit(solution)/shard_map/ppermute | solution.py:25
  146.4 2.3 collective-permute-start.2
  149.1 3.5 %collective-permute-start.3 = (f32[4,32,10,1]{1,0,3,2:T(4,128)S(1)}, f32[4,32,10,1]{1,0,3,2:T(4,128)S(1)}, u32[]{:S(2)}, u32[]{:S(2)}) collective-permute-start(f32[4,32,10,1]{1,0,3,2:T(4,128)S(1)} %copy.7), channel_id=1, source_target_pairs={{0,1},{1,2},{2,3},{3,4},{4,5},{5,6},{6,7},{8,9},{9,10},{10,11},{11... | collective-permute-start | bytes 15368 | tf_op jit(solution)/shard_map/ppermute | solution.py:25
  153.2 2.7 %collective-permute-done.3 = f32[4,32,10,1]{1,0,3,2:T(4,128)S(1)} collective-permute-done((f32[4,32,10,1]{1,0,3,2:T(4,128)S(1)}, f32[4,32,10,1]{1,0,3,2:T(4,128)S(1)}, u32[]{:S(2)}, u32[]{:S(2)}) %collective-permute-start.3) | collective-permute-done | bytes 5152 | tf_op jit(solution)/shard_map/ppermute | solution.py:25
  156.5 2.2 subtract_add_fusion.3
  158.7 0.7 reduce-window_multiply_fusion.3
  159.4 0.9 broadcast_multiply_fusion.6
  160.4 1.9 collective-permute-start.4
  162.4 2.4 collective-permute-start.5
  164.8 4.7 %collective-permute-done.5 = f32[4,32,1,128]{3,2,1,0:T(1,128)S(1)} collective-permute-done((f32[4,32,1,128]{3,2,1,0:T(1,128)S(1)}, f32[4,32,1,128]{3,2,1,0:T(1,128)S(1)}, u32[]{:S(2)}, u32[]{:S(2)}) %collective-permute-start.5) | collective-permute-done | bytes 65568 | tf_op jit(solution)/shard_map/ppermute | solution.py:25
  170.0 1.0 copy.11
  171.0 1.9 collective-permute-start.6
  173.3 3.9 %collective-permute-start.7 = (f32[4,32,10,1]{1,0,3,2:T(4,128)S(1)}, f32[4,32,10,1]{1,0,3,2:T(4,128)}, u32[]{:S(2)}, u32[]{:S(2)}) collective-permute-start(f32[4,32,10,1]{1,0,3,2:T(4,128)S(1)} %copy.13), channel_id=1, source_target_pairs={{0,1},{1,2},{2,3},{3,4},{4,5},{5,6},{6,7},{8,9},{9,10},{10,11},{11... | collective-permute-start | bytes 15368 | tf_op jit(solution)/shard_map/ppermute | solution.py:25
  177.2 0.9 fusion.68
  178.7 1.6 collective-permute-done.7
  180.3 1.2 copy.14
  181.5 2.2 subtract_add_fusion.2
  183.8 0.7 reduce-window_multiply_fusion.2
  184.9 1.9 collective-permute-start.8
  186.8 2.4 collective-permute-start.9
  189.2 4.7 %collective-permute-done.9 = f32[4,32,1,128]{3,2,1,0:T(1,128)S(1)} collective-permute-done((f32[4,32,1,128]{3,2,1,0:T(1,128)S(1)}, f32[4,32,1,128]{3,2,1,0:T(1,128)S(1)}, u32[]{:S(2)}, u32[]{:S(2)}) %collective-permute-start.9) | collective-permute-done | bytes 65568 | tf_op jit(solution)/shard_map/ppermute | solution.py:25
  194.1 1.3 fusion.130
  195.4 1.6 copy.17
  197.0 1.9 collective-permute-start.10
  199.3 4.1 %collective-permute-start.11 = (f32[4,32,10,1]{1,0,3,2:T(4,128)S(1)}, f32[4,32,10,1]{1,0,3,2:T(4,128)S(1)}, u32[]{:S(2)}, u32[]{:S(2)}) collective-permute-start(f32[4,32,10,1]{1,0,3,2:T(4,128)S(1)} %copy.19), channel_id=1, source_target_pairs={{0,1},{1,2},{2,3},{3,4},{4,5},{5,6},{6,7},{8,9},{9,10},{10,11},{11... | collective-permute-start | bytes 15368 | tf_op jit(solution)/shard_map/ppermute | solution.py:25
  203.4 0.9 fusion.67
  204.8 1.3 collective-permute-done.11
  206.7 2.1 subtract_add_fusion.1
  208.9 0.7 reduce-window_multiply_fusion.1
  209.6 0.9 broadcast_multiply_fusion.2
  210.6 1.9 collective-permute-start.12
  212.6 2.4 collective-permute-start.13
  215.0 4.7 %collective-permute-done.13 = f32[4,32,1,128]{3,2,1,0:T(1,128)S(1)} collective-permute-done((f32[4,32,1,128]{3,2,1,0:T(1,128)S(1)}, f32[4,32,1,128]{3,2,1,0:T(1,128)S(1)}, u32[]{:S(2)}, u32[]{:S(2)}) %collective-permute-start.13) | collective-permute-done | bytes 65568 | tf_op jit(solution)/shard_map/ppermute | solution.py:25
  220.2 1.0 copy.23
  221.2 1.9 collective-permute-start.14
  223.5 3.9 %collective-permute-start.15 = (f32[4,32,10,1]{1,0,3,2:T(4,128)S(1)}, f32[4,32,10,1]{1,0,3,2:T(4,128)}, u32[]{:S(2)}, u32[]{:S(2)}) collective-permute-start(f32[4,32,10,1]{1,0,3,2:T(4,128)S(1)} %copy.25), channel_id=1, source_target_pairs={{0,1},{1,2},{2,3},{3,4},{4,5},{5,6},{6,7},{8,9},{9,10},{10,11},{11... | collective-permute-start | bytes 15368 | tf_op jit(solution)/shard_map/ppermute | solution.py:25
  228.1 2.4 collective-permute-done.15
  230.5 1.2 copy.26
  231.8 1.8 subtract_add_fusion
  233.6 0.7 reduce-window_multiply_fusion
  234.6 0.8 maximum_bitcast_fusion
  (69 shorter events, 8.4 us)
Async XLA Ops:
  6.5 0.7 copy-start
  6.5 133.7 %copy-start.1 = (f32[31]{0:T(128)S(1)}, f32[31]{0:T(128)}, u32[]{:S(2)}) copy-start(f32[31]{0:T(128)} %param.9) | copy-start | bytes 376
  6.5 107.9 %all-gather.2.cloned.1.call-start = ((), (), s32[]{:S(2)}) async-start(), calls=%async_computation | async-start | bytes 8912896 | tf_op jit(solution)/shard_map/all_gather | solution.py:69
  134.5 6.7 %collective-permute-start = (f32[4,32,1,128]{3,2,1,0:T(1,128)S(1)}, f32[4,32,1,128]{3,2,1,0:T(1,128)S(1)}, u32[]{:S(2)}, u32[]{:S(2)}) collective-permute-start(f32[4,32,1,128]{3,2,1,0:T(1,128)S(1)} %get-tuple-element.148), channel_id=1, source_target_pairs={{8,0},{16,8},{24,16},{0,24},{9,1},{17,9},{25,17},{1,25},{10,2},{18... | collective-permute-start | bytes 196616 | tf_op jit(solution)/shard_map/ppermute | solution.py:26
  138.3 7.1 %collective-permute-start.1 = (f32[4,32,1,128]{3,2,1,0:T(1,128)S(1)}, f32[4,32,1,128]{3,2,1,0:T(1,128)S(1)}, u32[]{:S(2)}, u32[]{:S(2)}) collective-permute-start(f32[4,32,1,128]{3,2,1,0:T(1,128)S(1)} %get-tuple-element.147), channel_id=1, source_target_pairs={{0,8},{8,16},{16,24},{24,0},{1,9},{9,17},{17,25},{25,1},{2,10},{10... | collective-permute-start | bytes 196616 | tf_op jit(solution)/shard_map/ppermute | solution.py:25
  146.4 6.3 %collective-permute-start.2 = (f32[4,32,10,1]{1,0,3,2:T(4,128)S(1)}, f32[4,32,10,1]{1,0,3,2:T(4,128)S(1)}, u32[]{:S(2)}, u32[]{:S(2)}) collective-permute-start(f32[4,32,10,1]{1,0,3,2:T(4,128)S(1)} %copy.5), channel_id=1, source_target_pairs={{1,0},{2,1},{3,2},{4,3},{5,4},{6,5},{7,6},{9,8},{10,9},{11,10},{12... | collective-permute-start | bytes 15368 | tf_op jit(solution)/shard_map/ppermute | solution.py:26
  149.1 6.9 %collective-permute-start.3 = (f32[4,32,10,1]{1,0,3,2:T(4,128)S(1)}, f32[4,32,10,1]{1,0,3,2:T(4,128)S(1)}, u32[]{:S(2)}, u32[]{:S(2)}) collective-permute-start(f32[4,32,10,1]{1,0,3,2:T(4,128)S(1)} %copy.7), channel_id=1, source_target_pairs={{0,1},{1,2},{2,3},{3,4},{4,5},{5,6},{6,7},{8,9},{9,10},{10,11},{11... | collective-permute-start | bytes 15368 | tf_op jit(solution)/shard_map/ppermute | solution.py:25
  160.4 4.3 %collective-permute-start.4 = (f32[4,32,1,128]{3,2,1,0:T(1,128)S(1)}, f32[4,32,1,128]{3,2,1,0:T(1,128)S(1)}, u32[]{:S(2)}, u32[]{:S(2)}) collective-permute-start(f32[4,32,1,128]{3,2,1,0:T(1,128)S(1)} %get-tuple-element.144), channel_id=1, source_target_pairs={{8,0},{16,8},{24,16},{0,24},{9,1},{17,9},{25,17},{1,25},{10,2},{18... | collective-permute-start | bytes 196616 | tf_op jit(solution)/shard_map/ppermute | solution.py:26
  162.4 7.1 %collective-permute-start.5 = (f32[4,32,1,128]{3,2,1,0:T(1,128)S(1)}, f32[4,32,1,128]{3,2,1,0:T(1,128)S(1)}, u32[]{:S(2)}, u32[]{:S(2)}) collective-permute-start(f32[4,32,1,128]{3,2,1,0:T(1,128)S(1)} %get-tuple-element.143), channel_id=1, source_target_pairs={{0,8},{8,16},{16,24},{24,0},{1,9},{9,17},{17,25},{25,1},{2,10},{10... | collective-permute-start | bytes 196616 | tf_op jit(solution)/shard_map/ppermute | solution.py:25
  171.0 7.1 %collective-permute-start.6 = (f32[4,32,10,1]{1,0,3,2:T(4,128)}, f32[4,32,10,1]{1,0,3,2:T(4,128)S(1)}, u32[]{:S(2)}, u32[]{:S(2)}) collective-permute-start(f32[4,32,10,1]{1,0,3,2:T(4,128)} %copy.11), channel_id=1, source_target_pairs={{1,0},{2,1},{3,2},{4,3},{5,4},{6,5},{7,6},{9,8},{10,9},{11,10},{12... | collective-permute-start | bytes 15368 | tf_op jit(solution)/shard_map/ppermute | solution.py:26
  173.3 7.0 %collective-permute-start.7 = (f32[4,32,10,1]{1,0,3,2:T(4,128)S(1)}, f32[4,32,10,1]{1,0,3,2:T(4,128)}, u32[]{:S(2)}, u32[]{:S(2)}) collective-permute-start(f32[4,32,10,1]{1,0,3,2:T(4,128)S(1)} %copy.13), channel_id=1, source_target_pairs={{0,1},{1,2},{2,3},{3,4},{4,5},{5,6},{6,7},{8,9},{9,10},{10,11},{11... | collective-permute-start | bytes 15368 | tf_op jit(solution)/shard_map/ppermute | solution.py:25
  184.9 4.3 %collective-permute-start.8 = (f32[4,32,1,128]{3,2,1,0:T(1,128)S(1)}, f32[4,32,1,128]{3,2,1,0:T(1,128)S(1)}, u32[]{:S(2)}, u32[]{:S(2)}) collective-permute-start(f32[4,32,1,128]{3,2,1,0:T(1,128)S(1)} %get-tuple-element.142), channel_id=1, source_target_pairs={{8,0},{16,8},{24,16},{0,24},{9,1},{17,9},{25,17},{1,25},{10,2},{18... | collective-permute-start | bytes 196616 | tf_op jit(solution)/shard_map/ppermute | solution.py:26
  186.8 7.1 %collective-permute-start.9 = (f32[4,32,1,128]{3,2,1,0:T(1,128)S(1)}, f32[4,32,1,128]{3,2,1,0:T(1,128)S(1)}, u32[]{:S(2)}, u32[]{:S(2)}) collective-permute-start(f32[4,32,1,128]{3,2,1,0:T(1,128)S(1)} %get-tuple-element.141), channel_id=1, source_target_pairs={{0,8},{8,16},{16,24},{24,0},{1,9},{9,17},{17,25},{25,1},{2,10},{10... | collective-permute-start | bytes 196616 | tf_op jit(solution)/shard_map/ppermute | solution.py:25
  197.0 7.3 %collective-permute-start.10 = (f32[4,32,10,1]{1,0,3,2:T(4,128)S(1)}, f32[4,32,10,1]{1,0,3,2:T(4,128)S(1)}, u32[]{:S(2)}, u32[]{:S(2)}) collective-permute-start(f32[4,32,10,1]{1,0,3,2:T(4,128)S(1)} %copy.17), channel_id=1, source_target_pairs={{1,0},{2,1},{3,2},{4,3},{5,4},{6,5},{7,6},{9,8},{10,9},{11,10},{12... | collective-permute-start | bytes 15368 | tf_op jit(solution)/shard_map/ppermute | solution.py:26
  199.3 6.9 %collective-permute-start.11 = (f32[4,32,10,1]{1,0,3,2:T(4,128)S(1)}, f32[4,32,10,1]{1,0,3,2:T(4,128)S(1)}, u32[]{:S(2)}, u32[]{:S(2)}) collective-permute-start(f32[4,32,10,1]{1,0,3,2:T(4,128)S(1)} %copy.19), channel_id=1, source_target_pairs={{0,1},{1,2},{2,3},{3,4},{4,5},{5,6},{6,7},{8,9},{9,10},{10,11},{11... | collective-permute-start | bytes 15368 | tf_op jit(solution)/shard_map/ppermute | solution.py:25
  210.6 4.3 %collective-permute-start.12 = (f32[4,32,1,128]{3,2,1,0:T(1,128)S(1)}, f32[4,32,1,128]{3,2,1,0:T(1,128)S(1)}, u32[]{:S(2)}, u32[]{:S(2)}) collective-permute-start(f32[4,32,1,128]{3,2,1,0:T(1,128)S(1)} %get-tuple-element.140), channel_id=1, source_target_pairs={{8,0},{16,8},{24,16},{0,24},{9,1},{17,9},{25,17},{1,25},{10,2},{18... | collective-permute-start | bytes 196616 | tf_op jit(solution)/shard_map/ppermute | solution.py:26
  212.6 7.1 %collective-permute-start.13 = (f32[4,32,1,128]{3,2,1,0:T(1,128)S(1)}, f32[4,32,1,128]{3,2,1,0:T(1,128)S(1)}, u32[]{:S(2)}, u32[]{:S(2)}) collective-permute-start(f32[4,32,1,128]{3,2,1,0:T(1,128)S(1)} %get-tuple-element.139), channel_id=1, source_target_pairs={{0,8},{8,16},{16,24},{24,0},{1,9},{9,17},{17,25},{25,1},{2,10},{10... | collective-permute-start | bytes 196616 | tf_op jit(solution)/shard_map/ppermute | solution.py:25
  221.2 6.4 %collective-permute-start.14 = (f32[4,32,10,1]{1,0,3,2:T(4,128)}, f32[4,32,10,1]{1,0,3,2:T(4,128)S(1)}, u32[]{:S(2)}, u32[]{:S(2)}) collective-permute-start(f32[4,32,10,1]{1,0,3,2:T(4,128)} %copy.23), channel_id=1, source_target_pairs={{1,0},{2,1},{3,2},{4,3},{5,4},{6,5},{7,6},{9,8},{10,9},{11,10},{12... | collective-permute-start | bytes 15368 | tf_op jit(solution)/shard_map/ppermute | solution.py:26
  223.5 7.0 %collective-permute-start.15 = (f32[4,32,10,1]{1,0,3,2:T(4,128)S(1)}, f32[4,32,10,1]{1,0,3,2:T(4,128)}, u32[]{:S(2)}, u32[]{:S(2)}) collective-permute-start(f32[4,32,10,1]{1,0,3,2:T(4,128)S(1)} %copy.25), channel_id=1, source_target_pairs={{0,1},{1,2},{2,3},{3,4},{4,5},{5,6},{6,7},{8,9},{9,10},{10,11},{11... | collective-permute-start | bytes 15368 | tf_op jit(solution)/shard_map/ppermute | solution.py:25
Sparse Core Ops, SparseCore 0:
  9.4 104.9 all-gather.1
where the time goes:
time: 244 us; the launch traced here: 242 us
  waiting for transfers between devices  133 us (55%)
  starting transfers between devices  42.2 us (17%)
  other arithmetic  38.3 us (16%)
  local copies, waits for them, and re-layouts  14.2 us (6%)
  between operations  13.9 us (6%)
    all_gather x1, waiting for transfers between devices, per_device(): shards = lax.all_gather(ensemble, 'dom', axis=0, tiled=True)  106 us
    ppermute x8, waiting for transfers between devices, extended(): before = lax.ppermute(last, axis, up)  26.4 us
    ppermute x8, starting transfers between devices, extended(): before = lax.ppermute(last, axis, up)  24.6 us
    select_n x16, other arithmetic, place(): return jnp.where(wanted, shards[offset], partial_state)  19.4 us
    ppermute x8, starting transfers between devices, extended(): after = lax.ppermute(leading, axis, down)  17.6 us
    add x4, other arithmetic, advance(): common = centre - ADVECT * carried_over + DIFFUSE * spread + vertical  8.36 us
  transfers between devices with their start and end apart: 17, of which 9 were waited for; matrix products, arithmetic and copies ran while one was open for 3% of the time, Pallas kernels for 0%

commit v1 on v0

--- a/solution.py
+++ b/solution.py
@@ -2,6 +2,7 @@
 import jax.numpy as jnp
 from jax import lax
 from jax.sharding import PartitionSpec as P
+from jax.lax import all_to_all, axis_size
 
 STEPS = 4
 TILE = 8
@@ -66,7 +67,9 @@
     width_y = ensemble.shape[4]
     own_tiles = lax.dynamic_index_in_dim(ancestors, particle_number, 0, keepdims=False)
     cell_source = jnp.repeat(jnp.repeat(own_tiles, TILE, 0), TILE, 1)
-    shards = lax.all_gather(ensemble, "dom", axis=0, tiled=True)
+    a_now = jnp.stack([ensemble for _ in range(axis_size("dom"))])
+    formed = all_to_all(a_now, "dom", 0, 0)
+    shards = jnp.concatenate(formed, axis=0)
 
     def place(offset, partial_state):
         wanted = (cell_source == offset)[None, None]

time: 244 us -> 324 us (1.33)
  the two profiles are of different devices: /device:TPU:256 before, /device:TPU:296 now
where the time goes in v1:
time: 324 us; the launch traced here: 323 us
  waiting for transfers between devices  215 us (66%)
  starting transfers between devices  49.9 us (15%)
  other arithmetic  37.5 us (12%)
  local copies, waits for them, and re-layouts  19.5 us (6%)
    all_to_all x1, waiting for transfers between devices, per_device(): formed = all_to_all(a_now, 'dom', 0, 0)  189 us
    ppermute x8, waiting for transfers between devices, extended(): before = lax.ppermute(last, axis, up)  26 us
    ppermute x8, starting transfers between devices, extended(): before = lax.ppermute(last, axis, up)  25 us
    select_n x16, other arithmetic, place(): return jnp.where(wanted, shards[offset], partial_state)  19.4 us
    ppermute x8, starting transfers between devices, extended(): after = lax.ppermute(leading, axis, down)  16.8 us
    add x4, other arithmetic, advance(): common = centre - ADVECT * carried_over + DIFFUSE * spread + vertical  8.3 us
    all_to_all x1, starting transfers between devices, per_device(): formed = all_to_all(a_now, 'dom', 0, 0)  8.17 us
  transfers between devices with their start and end apart: 17, of which 9 were waited for; matrix products, arithmetic and copies ran while one was open for 2% of the time, Pallas kernels for 0%

profile of v1, /device:TPU:296, one launch (start us, length us, event | category | flops | bytes accessed | tf_op | source)
XLA Modules:
  0.0 322.5 jit_solution(6651523206507935797)
XLA Ops:
  0.0 5.3 %stack.59 = f32[16,1,4,32,8,128]{5,4,3,2,1,0:T(8,128)} broadcast(f32[4,32,8,128]{3,2,1,0:T(8,128)} %bitcast.150), dimensions={2,3,4,5} | broadcast | bytes 8912896 | tf_op jit(solution)/shard_map/stack | solution.py:70
  5.3 8.2 %all-to-all-start = ((f32[16,1,4,32,8,128]{5,4,3,2,1,0:T(8,128)}), f32[16,1,4,32,8,128]{5,4,3,2,1,0:T(8,128)}, u32[]{:S(2)}, u32[]{:S(2)}) async-start(f32[16,1,4,32,8,128]{5,4,3,2,1,0:T(8,128)} %stack.59), calls=%async_computation | async-start | bytes 16777216 | tf_op jit(solution)/shard_map/all_to_all | solution.py:71
  13.8 188.6 %all-to-all-done = f32[16,1,4,32,8,128]{5,4,3,2,1,0:T(8,128)} async-done(((f32[16,1,4,32,8,128]{5,4,3,2,1,0:T(8,128)}), f32[16,1,4,32,8,128]{5,4,3,2,1,0:T(8,128)}, u32[]{:S(2)}, u32[]{:S(2)}) %all-to-all-start) | async-done | bytes 8388640 | tf_op jit(solution)/shard_map/all_to_all | solution.py:71
  202.5 19.9 %while.14 = (s32[]{:T(128)}, f32[4,32,8,128]{3,2,1,0:T(8,128)S(1)}, f32[16,4,32,8,128]{4,3,2,1,0:T(8,128)}, s32[128]{0:T(128)S(1)}, s32[]{:T(128)}, /*index=5*/s32[]{:T(128)}) while((s32[]{:T(128)}, f32[4,32,8,128]{3,2,1,0:T(8,128)S(1)}, f32[16,4,32,8,128]{4,3,2,1,0:T(8,128)}, s32[128]{0:T(128)S(1)}, s32[]{:T(128)}, ...), condition=%wide.region_1.2_spmd.clone, body=%wide.region_0.1_spmd.clone.sunk | while | flops 262275 | bytes 1573719 | solution.py:78
  202.5 1.2 bitcast_select_fusion.2
  203.7 1.2 bitcast_select_fusion.2
  205.0 1.2 bitcast_select_fusion.2
  206.2 1.2 bitcast_select_fusion.2
  207.5 1.2 bitcast_select_fusion.2
  208.7 1.2 bitcast_select_fusion.2
  210.0 1.2 bitcast_select_fusion.2
  211.2 1.2 bitcast_select_fusion.2
  212.5 1.2 bitcast_select_fusion.2
  213.7 1.2 bitcast_select_fusion.2
  214.9 1.2 bitcast_select_fusion.2
  216.2 1.2 bitcast_select_fusion.2
  217.4 1.2 bitcast_select_fusion.2
  218.7 1.2 bitcast_select_fusion.2
  219.9 1.2 bitcast_select_fusion.2
  221.2 1.2 bitcast_select_fusion.2
  222.5 3.4 %collective-permute-start = (f32[4,32,1,128]{3,2,1,0:T(1,128)S(1)}, f32[4,32,1,128]{3,2,1,0:T(1,128)S(1)}, u32[]{:S(2)}, u32[]{:S(2)}) collective-permute-start(f32[4,32,1,128]{3,2,1,0:T(1,128)S(1)} %get-tuple-element.148), channel_id=1, source_target_pairs={{8,0},{16,8},{24,16},{0,24},{9,1},{17,9},{25,17},{1,25},{10,2},{18... | collective-permute-start | bytes 196616 | tf_op jit(solution)/shard_map/ppermute | solution.py:27
  225.9 1.9 collective-permute-start.1
  227.8 0.9 subtract_multiply_fusion
  228.7 4.3 %collective-permute-done.1 = f32[4,32,1,128]{3,2,1,0:T(1,128)S(1)} collective-permute-done((f32[4,32,1,128]{3,2,1,0:T(1,128)S(1)}, f32[4,32,1,128]{3,2,1,0:T(1,128)S(1)}, u32[]{:S(2)}, u32[]{:S(2)}) %collective-permute-start.1) | collective-permute-done | bytes 65568 | tf_op jit(solution)/shard_map/ppermute | solution.py:26
  233.9 1.9 collective-permute-start.2
  236.2 3.9 %collective-permute-start.3 = (f32[4,32,10,1]{1,0,3,2:T(4,128)S(1)}, f32[4,32,10,1]{1,0,3,2:T(4,128)S(1)}, u32[]{:S(2)}, u32[]{:S(2)}) collective-permute-start(f32[4,32,10,1]{1,0,3,2:T(4,128)S(1)} %copy.7), channel_id=1, source_target_pairs={{0,1},{1,2},{2,3},{3,4},{4,5},{5,6},{6,7},{8,9},{9,10},{10,11},{11... | collective-permute-start | bytes 15368 | tf_op jit(solution)/shard_map/ppermute | solution.py:26
  240.7 2.4 collective-permute-done.3
  243.7 2.1 subtract_add_fusion.3
  245.8 0.7 reduce-window_multiply_fusion.3
  246.6 0.9 broadcast_multiply_fusion.6
  247.6 1.9 collective-permute-start.4
  249.5 2.4 collective-permute-start.5
  252.0 4.7 %collective-permute-done.5 = f32[4,32,1,128]{3,2,1,0:T(1,128)S(1)} collective-permute-done((f32[4,32,1,128]{3,2,1,0:T(1,128)S(1)}, f32[4,32,1,128]{3,2,1,0:T(1,128)S(1)}, u32[]{:S(2)}, u32[]{:S(2)}) %collective-permute-start.5) | collective-permute-done | bytes 65568 | tf_op jit(solution)/shard_map/ppermute | solution.py:26
  257.2 1.0 copy.11
  258.1 1.9 collective-permute-start.6
  260.5 3.9 %collective-permute-start.7 = (f32[4,32,10,1]{1,0,3,2:T(4,128)S(1)}, f32[4,32,10,1]{1,0,3,2:T(4,128)}, u32[]{:S(2)}, u32[]{:S(2)}) collective-permute-start(f32[4,32,10,1]{1,0,3,2:T(4,128)S(1)} %copy.13), channel_id=1, source_target_pairs={{0,1},{1,2},{2,3},{3,4},{4,5},{5,6},{6,7},{8,9},{9,10},{10,11},{11... | collective-permute-start | bytes 15368 | tf_op jit(solution)/shard_map/ppermute | solution.py:26
  264.4 0.9 fusion.68
  265.8 1.6 collective-permute-done.7
  267.5 1.2 copy.14
  268.7 2.2 subtract_add_fusion.2
  270.9 0.7 reduce-window_multiply_fusion.2
  272.0 1.9 collective-permute-start.8
  273.9 2.4 collective-permute-start.9
  276.4 4.7 %collective-permute-done.9 = f32[4,32,1,128]{3,2,1,0:T(1,128)S(1)} collective-permute-done((f32[4,32,1,128]{3,2,1,0:T(1,128)S(1)}, f32[4,32,1,128]{3,2,1,0:T(1,128)S(1)}, u32[]{:S(2)}, u32[]{:S(2)}) %collective-permute-start.9) | collective-permute-done | bytes 65568 | tf_op jit(solution)/shard_map/ppermute | solution.py:26
  281.2 1.3 fusion.130
  282.5 1.6 copy.17
  284.1 1.9 collective-permute-start.10
  286.4 4.1 %collective-permute-start.11 = (f32[4,32,10,1]{1,0,3,2:T(4,128)S(1)}, f32[4,32,10,1]{1,0,3,2:T(4,128)S(1)}, u32[]{:S(2)}, u32[]{:S(2)}) collective-permute-start(f32[4,32,10,1]{1,0,3,2:T(4,128)S(1)} %copy.19), channel_id=1, source_target_pairs={{0,1},{1,2},{2,3},{3,4},{4,5},{5,6},{6,7},{8,9},{9,10},{10,11},{11... | collective-permute-start | bytes 15368 | tf_op jit(solution)/shard_map/ppermute | solution.py:26
  290.5 0.9 fusion.67
  292.0 1.3 collective-permute-done.11
  293.9 2.1 subtract_add_fusion.1
  296.0 0.7 reduce-window_multiply_fusion.1
  296.8 0.9 broadcast_multiply_fusion.2
  297.8 1.9 collective-permute-start.12
  299.7 2.4 collective-permute-start.13
  302.1 4.7 %collective-permute-done.13 = f32[4,32,1,128]{3,2,1,0:T(1,128)S(1)} collective-permute-done((f32[4,32,1,128]{3,2,1,0:T(1,128)S(1)}, f32[4,32,1,128]{3,2,1,0:T(1,128)S(1)}, u32[]{:S(2)}, u32[]{:S(2)}) %collective-permute-start.13) | collective-permute-done | bytes 65568 | tf_op jit(solution)/shard_map/ppermute | solution.py:26
  307.3 1.0 copy.23
  308.3 1.9 collective-permute-start.14
  310.6 3.9 %collective-permute-start.15 = (f32[4,32,10,1]{1,0,3,2:T(4,128)S(1)}, f32[4,32,10,1]{1,0,3,2:T(4,128)}, u32[]{:S(2)}, u32[]{:S(2)}) collective-permute-start(f32[4,32,10,1]{1,0,3,2:T(4,128)S(1)} %copy.25), channel_id=1, source_target_pairs={{0,1},{1,2},{2,3},{3,4},{4,5},{5,6},{6,7},{8,9},{9,10},{10,11},{11... | collective-permute-start | bytes 15368 | tf_op jit(solution)/shard_map/ppermute | solution.py:26
  315.2 2.4 collective-permute-done.15
  317.6 1.2 copy.26
  318.9 1.8 subtract_add_fusion
  320.8 0.7 reduce-window_multiply_fusion
  321.7 0.8 maximum_bitcast_fusion
  (71 shorter events, 8.4 us)
Async XLA Ops:
  0.0 13.5 %copy-start = (s32[16,1,16]{2,1,0:T(1,128)S(1)}, s32[16,1,16]{2,1,0:T(1,128)}, u32[]{:S(2)}) copy-start(s32[16,1,16]{2,1,0:T(1,128)} %param.7) | copy-start | bytes 3076
  5.3 8.4 %copy-start.2 = (f32[1,2,8,128]{3,2,1,0:T(8,128)S(1)}, f32[1,2,8,128]{3,2,1,0:T(8,128)}, u32[]{:S(2)}) copy-start(f32[1,2,8,128]{3,2,1,0:T(8,128)} %param.8) | copy-start | bytes 24580
  5.3 197.2 %all-to-all-start = ((f32[16,1,4,32,8,128]{5,4,3,2,1,0:T(8,128)}), f32[16,1,4,32,8,128]{5,4,3,2,1,0:T(8,128)}, u32[]{:S(2)}, u32[]{:S(2)}) async-start(f32[16,1,4,32,8,128]{5,4,3,2,1,0:T(8,128)} %stack.59), calls=%async_computation | async-start | bytes 16777216 | tf_op jit(solution)/shard_map/all_to_all | solution.py:71
  13.5 214.3 %copy-start.1 = (f32[31]{0:T(128)S(1)}, f32[31]{0:T(128)}, u32[]{:S(2)}) copy-start(f32[31]{0:T(128)} %param.9) | copy-start | bytes 376
  222.5 6.2 %collective-permute-start = (f32[4,32,1,128]{3,2,1,0:T(1,128)S(1)}, f32[4,32,1,128]{3,2,1,0:T(1,128)S(1)}, u32[]{:S(2)}, u32[]{:S(2)}) collective-permute-start(f32[4,32,1,128]{3,2,1,0:T(1,128)S(1)} %get-tuple-element.148), channel_id=1, source_target_pairs={{8,0},{16,8},{24,16},{0,24},{9,1},{17,9},{25,17},{1,25},{10,2},{18... | collective-permute-start | bytes 196616 | tf_op jit(solution)/shard_map/ppermute | solution.py:27
  225.9 7.1 %collective-permute-start.1 = (f32[4,32,1,128]{3,2,1,0:T(1,128)S(1)}, f32[4,32,1,128]{3,2,1,0:T(1,128)S(1)}, u32[]{:S(2)}, u32[]{:S(2)}) collective-permute-start(f32[4,32,1,128]{3,2,1,0:T(1,128)S(1)} %get-tuple-element.147), channel_id=1, source_target_pairs={{0,8},{8,16},{16,24},{24,0},{1,9},{9,17},{17,25},{25,1},{2,10},{10... | collective-permute-start | bytes 196616 | tf_op jit(solution)/shard_map/ppermute | solution.py:26
  233.9 6.3 %collective-permute-start.2 = (f32[4,32,10,1]{1,0,3,2:T(4,128)S(1)}, f32[4,32,10,1]{1,0,3,2:T(4,128)S(1)}, u32[]{:S(2)}, u32[]{:S(2)}) collective-permute-start(f32[4,32,10,1]{1,0,3,2:T(4,128)S(1)} %copy.5), channel_id=1, source_target_pairs={{1,0},{2,1},{3,2},{4,3},{5,4},{6,5},{7,6},{9,8},{10,9},{11,10},{12... | collective-permute-start | bytes 15368 | tf_op jit(solution)/shard_map/ppermute | solution.py:27
  236.2 6.9 %collective-permute-start.3 = (f32[4,32,10,1]{1,0,3,2:T(4,128)S(1)}, f32[4,32,10,1]{1,0,3,2:T(4,128)S(1)}, u32[]{:S(2)}, u32[]{:S(2)}) collective-permute-start(f32[4,32,10,1]{1,0,3,2:T(4,128)S(1)} %copy.7), channel_id=1, source_target_pairs={{0,1},{1,2},{2,3},{3,4},{4,5},{5,6},{6,7},{8,9},{9,10},{10,11},{11... | collective-permute-start | bytes 15368 | tf_op jit(solution)/shard_map/ppermute | solution.py:26
  247.6 4.3 %collective-permute-start.4 = (f32[4,32,1,128]{3,2,1,0:T(1,128)S(1)}, f32[4,32,1,128]{3,2,1,0:T(1,128)S(1)}, u32[]{:S(2)}, u32[]{:S(2)}) collective-permute-start(f32[4,32,1,128]{3,2,1,0:T(1,128)S(1)} %get-tuple-element.144), channel_id=1, source_target_pairs={{8,0},{16,8},{24,16},{0,24},{9,1},{17,9},{25,17},{1,25},{10,2},{18... | collective-permute-start | bytes 196616 | tf_op jit(solution)/shard_map/ppermute | solution.py:27
  249.5 7.1 %collective-permute-start.5 = (f32[4,32,1,128]{3,2,1,0:T(1,128)S(1)}, f32[4,32,1,128]{3,2,1,0:T(1,128)S(1)}, u32[]{:S(2)}, u32[]{:S(2)}) collective-permute-start(f32[4,32,1,128]{3,2,1,0:T(1,128)S(1)} %get-tuple-element.143), channel_id=1, source_target_pairs={{0,8},{8,16},{16,24},{24,0},{1,9},{9,17},{17,25},{25,1},{2,10},{10... | collective-permute-start | bytes 196616 | tf_op jit(solution)/shard_map/ppermute | solution.py:26
  258.1 7.1 %collective-permute-start.6 = (f32[4,32,10,1]{1,0,3,2:T(4,128)}, f32[4,32,10,1]{1,0,3,2:T(4,128)S(1)}, u32[]{:S(2)}, u32[]{:S(2)}) collective-permute-start(f32[4,32,10,1]{1,0,3,2:T(4,128)} %copy.11), channel_id=1, source_target_pairs={{1,0},{2,1},{3,2},{4,3},{5,4},{6,5},{7,6},{9,8},{10,9},{11,10},{12... | collective-permute-start | bytes 15368 | tf_op jit(solution)/shard_map/ppermute | solution.py:27
  260.5 7.0 %collective-permute-start.7 = (f32[4,32,10,1]{1,0,3,2:T(4,128)S(1)}, f32[4,32,10,1]{1,0,3,2:T(4,128)}, u32[]{:S(2)}, u32[]{:S(2)}) collective-permute-start(f32[4,32,10,1]{1,0,3,2:T(4,128)S(1)} %copy.13), channel_id=1, source_target_pairs={{0,1},{1,2},{2,3},{3,4},{4,5},{5,6},{6,7},{8,9},{9,10},{10,11},{11... | collective-permute-start | bytes 15368 | tf_op jit(solution)/shard_map/ppermute | solution.py:26
  272.0 4.3 %collective-permute-start.8 = (f32[4,32,1,128]{3,2,1,0:T(1,128)S(1)}, f32[4,32,1,128]{3,2,1,0:T(1,128)S(1)}, u32[]{:S(2)}, u32[]{:S(2)}) collective-permute-start(f32[4,32,1,128]{3,2,1,0:T(1,128)S(1)} %get-tuple-element.142), channel_id=1, source_target_pairs={{8,0},{16,8},{24,16},{0,24},{9,1},{17,9},{25,17},{1,25},{10,2},{18... | collective-permute-start | bytes 196616 | tf_op jit(solution)/shard_map/ppermute | solution.py:27
  273.9 7.1 %collective-permute-start.9 = (f32[4,32,1,128]{3,2,1,0:T(1,128)S(1)}, f32[4,32,1,128]{3,2,1,0:T(1,128)S(1)}, u32[]{:S(2)}, u32[]{:S(2)}) collective-permute-start(f32[4,32,1,128]{3,2,1,0:T(1,128)S(1)} %get-tuple-element.141), channel_id=1, source_target_pairs={{0,8},{8,16},{16,24},{24,0},{1,9},{9,17},{17,25},{25,1},{2,10},{10... | collective-permute-start | bytes 196616 | tf_op jit(solution)/shard_map/ppermute | solution.py:26
  284.1 7.3 %collective-permute-start.10 = (f32[4,32,10,1]{1,0,3,2:T(4,128)S(1)}, f32[4,32,10,1]{1,0,3,2:T(4,128)S(1)}, u32[]{:S(2)}, u32[]{:S(2)}) collective-permute-start(f32[4,32,10,1]{1,0,3,2:T(4,128)S(1)} %copy.17), channel_id=1, source_target_pairs={{1,0},{2,1},{3,2},{4,3},{5,4},{6,5},{7,6},{9,8},{10,9},{11,10},{12... | collective-permute-start | bytes 15368 | tf_op jit(solution)/shard_map/ppermute | solution.py:27
  286.4 6.9 %collective-permute-start.11 = (f32[4,32,10,1]{1,0,3,2:T(4,128)S(1)}, f32[4,32,10,1]{1,0,3,2:T(4,128)S(1)}, u32[]{:S(2)}, u32[]{:S(2)}) collective-permute-start(f32[4,32,10,1]{1,0,3,2:T(4,128)S(1)} %copy.19), channel_id=1, source_target_pairs={{0,1},{1,2},{2,3},{3,4},{4,5},{5,6},{6,7},{8,9},{9,10},{10,11},{11... | collective-permute-start | bytes 15368 | tf_op jit(solution)/shard_map/ppermute | solution.py:26
  297.8 4.3 %collective-permute-start.12 = (f32[4,32,1,128]{3,2,1,0:T(1,128)S(1)}, f32[4,32,1,128]{3,2,1,0:T(1,128)S(1)}, u32[]{:S(2)}, u32[]{:S(2)}) collective-permute-start(f32[4,32,1,128]{3,2,1,0:T(1,128)S(1)} %get-tuple-element.140), channel_id=1, source_target_pairs={{8,0},{16,8},{24,16},{0,24},{9,1},{17,9},{25,17},{1,25},{10,2},{18... | collective-permute-start | bytes 196616 | tf_op jit(solution)/shard_map/ppermute | solution.py:27
  299.7 7.1 %collective-permute-start.13 = (f32[4,32,1,128]{3,2,1,0:T(1,128)S(1)}, f32[4,32,1,128]{3,2,1,0:T(1,128)S(1)}, u32[]{:S(2)}, u32[]{:S(2)}) collective-permute-start(f32[4,32,1,128]{3,2,1,0:T(1,128)S(1)} %get-tuple-element.139), channel_id=1, source_target_pairs={{0,8},{8,16},{16,24},{24,0},{1,9},{9,17},{17,25},{25,1},{2,10},{10... | collective-permute-start | bytes 196616 | tf_op jit(solution)/shard_map/ppermute | solution.py:26
  308.3 6.4 %collective-permute-start.14 = (f32[4,32,10,1]{1,0,3,2:T(4,128)}, f32[4,32,10,1]{1,0,3,2:T(4,128)S(1)}, u32[]{:S(2)}, u32[]{:S(2)}) collective-permute-start(f32[4,32,10,1]{1,0,3,2:T(4,128)} %copy.23), channel_id=1, source_target_pairs={{1,0},{2,1},{3,2},{4,3},{5,4},{6,5},{7,6},{9,8},{10,9},{11,10},{12... | collective-permute-start | bytes 15368 | tf_op jit(solution)/shard_map/ppermute | solution.py:27
  310.6 7.0 %collective-permute-start.15 = (f32[4,32,10,1]{1,0,3,2:T(4,128)S(1)}, f32[4,32,10,1]{1,0,3,2:T(4,128)}, u32[]{:S(2)}, u32[]{:S(2)}) collective-permute-start(f32[4,32,10,1]{1,0,3,2:T(4,128)S(1)} %copy.25), channel_id=1, source_target_pairs={{0,1},{1,2},{2,3},{3,4},{4,5},{5,6},{6,7},{8,9},{9,10},{10,11},{11... | collective-permute-start | bytes 15368 | tf_op jit(solution)/shard_map/ppermute | solution.py:26
